TPU v7x, 32 devices: a whole 2x2x4 slice. The times are simulated.
32 devices in a mesh: section: 8 (over z, core), tensor: 4 (over y, x).
Axes of the slice: x: 2, y: 2, z: 4, core: 2. Of those that a mesh axis runs over, the one named last changes fastest.
Arguments:
- fwd_input: float32 [8, 256, 1024], P('section', 'tensor'), may hold values from -6 to 6
- out_grad: float32 [8, 256, 1024], P('section', 'tensor'), may hold values from -6 to 6
- w_inner: float32 [8, 1024, 16384], P('section', None, 'tensor'), may hold values from -0.1875 to 0.1875
- w_outer: float32 [8, 16384, 1024], P('section', 'tensor'), may hold values from -0.046875 to 0.046875
- lent_saved: float32 [8, 256, 16384], P('section', None, 'tensor'), may hold values from -6 to 6
Outputs:
- fwd_output: float32 [8, 256, 1024], P('section', 'tensor')
- in_grad: float32 [8, 256, 1024], P('section', 'tensor')
- lent_new: float32 [8, 256, 16384], P('section', None, 'tensor')
All inputs are finite; a program needn't handle non-finite values.
Results may differ from a plain program's by a relative error of at most 0.00007.
Values sent between devices are 32-bit elements; how exact they have to be, the bound alone decides.
A program may use at most 128 MiB of HBM per device.

v0:
```python
import jax
import jax.numpy as jnp
from jax import lax
from jax.sharding import PartitionSpec as P


def from_partner(value, axis, distance):
    mask = 2**distance
    pairs = [(source, source ^ mask) for source in range(lax.axis_size(axis))]
    return lax.ppermute(value, axis, pairs)


def from_behind(value, axis, by):
    length = lax.axis_size(axis)
    return lax.ppermute(value, axis, [(i, (i + by) % length) for i in range(length)])


def gelu_exact(value):
    return 0.5 * value * (1.0 + jax.scipy.special.erf(value / jnp.sqrt(2.0).astype(value.dtype)))


def gelu_slope(value):
    cumul = 0.5 * (1.0 + jax.scipy.special.erf(value / jnp.sqrt(2.0).astype(value.dtype)))
    dense = jnp.exp(-0.5 * value * value) / jnp.sqrt(2.0 * jnp.pi).astype(value.dtype)
    return cumul + value * dense


def forward_pass(x_rows, w_first, w_second):
    pre = jnp.dot(
        lax.all_gather(x_rows, "tensor", axis=0, tiled=True),
        w_first,
        precision=lax.Precision.HIGHEST,
        preferred_element_type=jnp.float32,
    )
    active = gelu_exact(pre)
    summed = lax.psum_scatter(
        jnp.dot(
            active, w_second, precision=lax.Precision.HIGHEST, preferred_element_type=jnp.float32
        ),
        "tensor",
        scatter_dimension=0,
        tiled=True,
    )
    return (x_rows + summed, pre)


def backward_pass(g_rows, w_first, w_second, old_pre):
    d_act = lax.dot_general(
        lax.all_gather(g_rows, "tensor", axis=0, tiled=True),
        w_second,
        (((1,), (1,)), ((), ())),
        precision=lax.Precision.HIGHEST,
        preferred_element_type=jnp.float32,
    )
    d_pre = d_act * gelu_slope(old_pre)
    summed = lax.psum_scatter(
        lax.dot_general(
            d_pre,
            w_first,
            (((1,), (1,)), ((), ())),
            precision=lax.Precision.HIGHEST,
            preferred_element_type=jnp.float32,
        ),
        "tensor",
        scatter_dimension=0,
        tiled=True,
    )
    return g_rows + summed


def shards(fwd_input, out_grad, w_inner, w_outer, lent_saved):
    x_rows = fwd_input[0]
    g_rows = out_grad[0]
    w_first = w_inner[0]
    w_second = w_outer[0]
    held = lent_saved[0]
    top_bit = lax.axis_size("section").bit_length() - 2
    out, pre = forward_pass(x_rows, w_first, w_second)
    given, old_pre = from_partner((pre, held), "section", top_bit)
    grad = backward_pass(g_rows, w_first, w_second, old_pre)
    moved_out = from_behind(out, "section", 1)
    moved_grad = from_behind(grad, "section", -1)
    return (moved_out[None], moved_grad[None], given[None])


def solution(mesh):
    return jax.shard_map(
        shards,
        mesh=mesh,
        in_specs=(
            P("section", "tensor", None),
            P("section", "tensor", None),
            P("section", None, "tensor"),
            P("section", "tensor", None),
            P("section", None, "tensor"),
        ),
        out_specs=(
            P("section", "tensor", None),
            P("section", "tensor", None),
            P("section", None, "tensor"),
        ),
        check_vma=False,
    )
```

profile of v0, /device:TPU:1, one launch (start us, length us, event | category | flops | bytes accessed | tf_op | source)
XLA Modules:
  0.0 390.0 jit_solution(11767922997621799056)
XLA Ops:
  7.2 0.0 all-gather.5.cloned.1.call-start
  7.2 0.7 all-gather.5.cloned.1.call-update
  7.9 0.0 all-gather.7.cloned.1.call-start
  7.9 3.2 collective-permute-start.1
  11.1 0.0 all-gather.7.cloned.1.call-update
  11.2 0.0 reduce-scatter.3.cloned.1.call-start
  11.2 27.0 %all-gather.5.cloned.1.call-done = f32[1,256,1024]{2,1,0:T(8,128)} async-done(((f32[1,64,1024]{2,1,0:T(8,128)}), f32[1,256,1024]{2,1,0:T(8,128)}) %all-gather.5.cloned.1.call-update) | async-done | bytes 1048592 | tf_op jit(solution)/shard_map/all_gather | solution.py:30
  38.3 0.0 copy-start
  38.3 18.4 %fusion.6 = f32[256,4096]{1,0:T(8,128)} fusion(f32[1,1024,4096]{2,1,0:T(8,128)} %param.7, f32[1,256,1024]{2,1,0:T(8,128)} %all-gather.5.cloned.1.call-done), kind=kOutput, calls=%fused_computation.6 | convolution fusion | flops 12884901888 | bytes 22020096 | tf_op jit(solution)/shard_map/dot_general | solution.py:29
  56.7 2.1 collective-permute-start.3
  58.8 0.0 copy-done
  58.8 21.1 %fusion.2 = f32[256,1024]{1,0:T(8,128)} fusion(f32[1,4096,1024]{2,1,0:T(8,128)S(1)} %copy-done, f32[256,4096]{1,0:T(8,128)} %fusion.6), kind=kOutput, calls=%fused_computation.2 | convolution fusion | flops 12889096192 | bytes 22020096 | tf_op jit(solution)/shard_map/dot_general | solution.py:37
  79.9 0.0 reduce-scatter.3.cloned.1.call-update
  79.9 0.0 reduce-scatter.5.cloned.1.call-start
  80.0 0.0 all-gather.7.cloned.1.call-done
  80.0 17.7 %fusion = f32[256,4096]{1,0:T(8,128)S(1)} fusion(f32[1,4096,1024]{2,1,0:T(8,128)} %param.8, f32[1,256,1024]{2,1,0:T(8,128)} %all-gather.7.cloned.1.call-done), kind=kOutput, calls=%fused_computation | convolution fusion | flops 12884901888 | bytes 22020096 | tf_op jit(solution)/shard_map/dot_general | solution.py:48
  97.7 0.0 copy-start.1
  97.7 0.0 copy-start.2
  97.7 183.8 %collective-permute-done.1 = f32[256,4096]{1,0:T(8,128)} collective-permute-done((f32[256,4096]{1,0:T(8,128)}, f32[256,4096]{1,0:T(8,128)}, u32[]{:S(2)}, u32[]{:S(2)}) %collective-permute-start.1) | collective-permute-done | bytes 4194336 | tf_op jit(solution)/shard_map/ppermute | solution.py:10
  281.5 22.7 %fusion.4 = f32[256,1024]{1,0:T(8,128)} fusion(f32[1,1024,4096]{2,1,0:T(8,128)} %param.7, f32[256,4096]{1,0:T(8,128)S(1)} %fusion, f32[256,4096]{1,0:T(8,128)} %collective-permute-done.1), kind=kOutput, calls=%fused_computation.4 | convolution fusion | flops 12894339072 | bytes 26214400 | tf_op jit(solution)/shard_map/dot_general | solution.py:57
  304.2 0.0 reduce-scatter.5.cloned.1.call-update
  304.2 0.0 reduce-scatter.3.cloned.1.call-done
  304.3 0.0 copy-done.1
  304.3 1.0 bitcast_add_fusion.1
  305.3 1.7 collective-permute-start
  307.0 27.0 %reduce-scatter.5.cloned.1.call-done = f32[64,1024]{1,0:T(8,128)} async-done(((f32[256,1024]{1,0:T(8,128)}), f32[64,1024]{1,0:T(8,128)}) %reduce-scatter.5.cloned.1.call-update) | async-done | bytes 262160 | tf_op jit(solution)/shard_map/reduce_scatter | solution.py:56
  334.0 0.0 copy-done.2
  334.0 1.0 bitcast_add_fusion
  335.0 0.9 collective-permute-start.2
  335.9 0.0 collective-permute-done
  335.9 38.3 %collective-permute-done.3 = f32[256,4096]{1,0:T(8,128)} collective-permute-done((f32[256,4096]{1,0:T(8,128)}, f32[256,4096]{1,0:T(8,128)}, u32[]{:S(2)}, u32[]{:S(2)}) %collective-permute-start.3) | collective-permute-done | bytes 4194336 | tf_op jit(solution)/shard_map/ppermute | solution.py:10
  374.2 3.2 collective-permute-done.2
  377.5 0.7 copy.11
  378.2 0.7 copy.12
  378.9 4.7 %copy.13 = f32[1,256,4096]{2,1,0:T(8,128)} copy(f32[1,256,4096]{2,1,0:T(8,128)} %bitcast.9) | data formatting | bytes 8388608
Async XLA Ops:
  7.2 31.1 %all-gather.5.cloned.1.call-start = ((), (), s32[]{:S(2)}) async-start(), calls=%async_computation.4 | async-start | bytes 1310720 | tf_op jit(solution)/shard_map/all_gather | solution.py:30
  7.9 72.1 %all-gather.7.cloned.1.call-start = ((), (), s32[]{:S(2)}) async-start(), calls=%async_computation.5 | async-start | bytes 1310720 | tf_op jit(solution)/shard_map/all_gather | solution.py:49
  7.9 273.6 %collective-permute-start.1 = (f32[256,4096]{1,0:T(8,128)}, f32[256,4096]{1,0:T(8,128)}, u32[]{:S(2)}, u32[]{:S(2)}) collective-permute-start(f32[256,4096]{1,0:T(8,128)} %bitcast.26), channel_id=1, source_target_pairs={{0,16},{4,20},{8,24},{12,28},{16,0},{20,4},{24,8},{28,12},{1,17},{... | collective-permute-start | bytes 12582920 | tf_op jit(solution)/shard_map/ppermute | solution.py:10
  11.2 293.1 %reduce-scatter.3.cloned.1.call-start = ((), (), s32[]{:S(2)}) async-start(), calls=%async_computation.2 | async-start | bytes 1310720 | tf_op jit(solution)/shard_map/reduce_scatter | solution.py:36
  38.3 20.5 %copy-start = (f32[1,4096,1024]{2,1,0:T(8,128)S(1)}, f32[1,4096,1024]{2,1,0:T(8,128)}, u32[]{:S(2)}) copy-start(f32[1,4096,1024]{2,1,0:T(8,128)} %param.8) | copy-start | bytes 50331652
  56.7 317.6 %collective-permute-start.3 = (f32[256,4096]{1,0:T(8,128)}, f32[256,4096]{1,0:T(8,128)}, u32[]{:S(2)}, u32[]{:S(2)}) collective-permute-start(f32[256,4096]{1,0:T(8,128)} %fusion.6), channel_id=1, source_target_pairs={{0,16},{4,20},{8,24},{12,28},{16,0},{20,4},{24,8},{28,12},{1,17},{... | collective-permute-start | bytes 12582920 | tf_op jit(solution)/shard_map/ppermute | solution.py:10
  79.9 254.1 %reduce-scatter.5.cloned.1.call-start = ((), (), s32[]{:S(2)}) async-start(), calls=%async_computation.3 | async-start | bytes 1310720 | tf_op jit(solution)/shard_map/reduce_scatter | solution.py:56
  97.7 206.5 %copy-start.1 = (f32[1,64,1024]{2,1,0:T(8,128)S(1)}, f32[1,64,1024]{2,1,0:T(8,128)}, u32[]{:S(2)}) copy-start(f32[1,64,1024]{2,1,0:T(8,128)} %param.5) | copy-start | bytes 786436
  97.7 236.3 %copy-start.2 = (f32[1,64,1024]{2,1,0:T(8,128)S(1)}, f32[1,64,1024]{2,1,0:T(8,128)}, u32[]{:S(2)}) copy-start(f32[1,64,1024]{2,1,0:T(8,128)} %param.6) | copy-start | bytes 786436
  305.3 30.6 %collective-permute-start = (f32[64,1024]{1,0:T(8,128)S(1)}, f32[64,1024]{1,0:T(8,128)S(1)}, u32[]{:S(2)}, u32[]{:S(2)}) collective-permute-start(f32[64,1024]{1,0:T(8,128)S(1)} %bitcast_add_fusion.1), channel_id=1, source_target_pairs={{0,4},{4,8},{8,12},{12,16},{16,20},{20,24},{24,28},{28,0},{1,5},{5... | collective-permute-start | bytes 786440 | tf_op jit(solution)/shard_map/ppermute | solution.py:15
  335.0 42.4 %collective-permute-start.2 = (f32[64,1024]{1,0:T(8,128)S(1)}, f32[64,1024]{1,0:T(8,128)S(1)}, u32[]{:S(2)}, u32[]{:S(2)}) collective-permute-start(f32[64,1024]{1,0:T(8,128)S(1)} %bitcast_add_fusion), channel_id=1, source_target_pairs={{0,28},{4,0},{8,4},{12,8},{16,12},{20,16},{24,20},{28,24},{1,29},{... | collective-permute-start | bytes 786440 | tf_op jit(solution)/shard_map/ppermute | solution.py:15
Sparse Core Ops, SparseCore 0:
  9.8 28.3 all-gather.4
  40.1 26.4 all-gather.6
  80.1 26.4 reduce-scatter.2
  304.4 29.6 reduce-scatter.4
where the time goes:
time: 390 us
  waiting for transfers between devices  280 us (72%)
  matrix products  79.9 us (20%)
  between operations  13.8 us (4%)
  starting transfers between devices  8.09 us (2%)
  local copies, waits for them, and re-layouts  6.07 us (2%)
    ppermute x2, waiting for transfers between devices, from_partner(): return lax.ppermute(value, axis, pairs)  222 us
    reduce_scatter x1, waiting for transfers between devices, backward_pass(): lax.psum_scatter(lax.dot_general(d_pre, w_first, (((1,), (1,)), ((), ()))...  27 us
    all_gather x1, waiting for transfers between devices, forward_pass(): lax.all_gather(x_rows, 'tensor', axis=0, tiled=True)  27 us
    dot_general x1, matrix products, backward_pass(): lax.dot_general(d_pre, w_first, (((1,), (1,)), ((), ())), precision=lax.P...  22.7 us
    dot_general x1, matrix products, forward_pass(): jnp.dot(active, w_second, precision=lax.Precision.HIGHEST, preferred_elem...  21.1 us
    dot_general x1, matrix products, forward_pass(): jnp.dot(lax.all_gather(x_rows, 'tensor', axis=0, tiled=True), w_first, pr...  18.4 us
    dot_general x1, matrix products, backward_pass(): lax.dot_general(lax.all_gather(g_rows, 'tensor', axis=0, tiled=True), w_s...  17.7 us
  transfers between devices with their start and end apart: 8, of which 5 were waited for; matrix products, arithmetic and copies ran while one was open for 21% of the time, Pallas kernels for 0%

commit v1 on v0

v1 whole, which is shorter than its diff:
```python
import functools

import jax
import jax.numpy as jnp
from jax import lax
from jax.experimental import pallas as pl
from jax.experimental.pallas import tpu as pltpu
from jax.sharding import PartitionSpec as P


OLD_EIGHTHS = (1, 3, 2, 2)
NEW_EIGHTHS = (3, 2, 2, 1)


def across(value, axis, mask):
    pairs = [(source, source ^ mask) for source in range(lax.axis_size(axis))]
    return lax.ppermute(value, axis, pairs)


def from_behind(value, axis, by):
    length = lax.axis_size(axis)
    return lax.ppermute(value, axis, [(i, (i + by) % length) for i in range(length)])


def gelu_exact(value):
    return 0.5 * value * (1.0 + jax.scipy.special.erf(value / jnp.sqrt(2.0).astype(value.dtype)))


def gelu_slope(value):
    cumul = 0.5 * (1.0 + jax.scipy.special.erf(value / jnp.sqrt(2.0).astype(value.dtype)))
    dense = jnp.exp(-0.5 * value * value) / jnp.sqrt(2.0 * jnp.pi).astype(value.dtype)
    return cumul + value * dense


def product(left, right, contract):
    return lax.dot_general(
        left,
        right,
        (contract, ((), ())),
        precision=lax.Precision.HIGHEST,
        preferred_element_type=jnp.float32,
    )


def gather_rows(rows, axis):
    count = lax.axis_size(axis)
    me = lax.axis_index(axis)
    pair, size, width = rows.shape
    whole = jnp.zeros((pair, count * size, width), rows.dtype)
    for d in range(count):
        part = rows if d == 0 else across(rows, axis, d)
        whole = lax.dynamic_update_slice(whole, part, (0, (me ^ d) * size, 0))
    return whole


def scatter_sum(whole, axis):
    count = lax.axis_size(axis)
    me = lax.axis_index(axis)
    size = whole.shape[0] // count
    total = lax.dynamic_slice(whole, (me * size, 0), (size, whole.shape[1]))
    for d in range(1, count):
        part = lax.dynamic_slice(whole, ((me ^ d) * size, 0), (size, whole.shape[1]))
        total = total + across(part, axis, d)
    return total


def moved(value, by):
    half = value.shape[0] // 2
    parts = [from_behind(value[:half], "section", by), from_behind(value[half:], "section", by)]
    return jnp.concatenate(lax.optimization_barrier(parts), axis=0)


def cuts(rows, eighths):
    starts, at = [], 0
    for n in eighths:
        size = rows * n // 8
        starts.append((at, size))
        at += size
    return starts


def put_kernel(at, *refs):
    part, out, sem = refs[-3:]
    copy = pltpu.make_async_copy(part, out.at[0, pl.ds(at, part.shape[0])], sem)
    copy.start()
    copy.wait()


def put(whole, part, at, shape):
    anywhere = pl.BlockSpec(memory_space=pl.ANY)
    held = () if whole is None else (whole,)
    return pl.pallas_call(
        functools.partial(put_kernel, at),
        out_shape=jax.ShapeDtypeStruct(shape, part.dtype),
        in_specs=[anywhere] * len(held) + [pl.BlockSpec(memory_space=pltpu.VMEM)],
        out_specs=anywhere,
        scratch_shapes=[pltpu.SemaphoreType.DMA],
        input_output_aliases={0: 0} if held else {},
        cost_estimate=pl.CostEstimate(flops=0, bytes_accessed=2 * part.size * 4, transcendentals=0),
    )(*held, part)


def shards(fwd_input, out_grad, w_inner, w_outer, lent_saved):
    x_rows = fwd_input[0]
    g_rows = out_grad[0]
    w_first = w_inner[0]
    w_second = w_outer[0]
    held = lent_saved[0]
    mask = lax.axis_size("section") // 2
    rows, width = held.shape
    barrier = lax.optimization_barrier

    old = []
    for i, (at, size) in enumerate(cuts(rows, OLD_EIGHTHS)):
        piece = held[at : at + size]
        if i == 0:
            piece, held = barrier((piece, held))
        old.append(across(piece, "section", mask))

    both = gather_rows(jnp.stack([x_rows, g_rows]), "tensor")

    pre = product(both[0], w_first, ((1,), (0,)))
    summed = scatter_sum(product(gelu_exact(pre), w_second, ((1,), (0,))), "tensor")
    moved_out = moved(x_rows + summed, 1)

    d_act = product(both[1], w_second, ((1,), (1,)))
    d_pre = d_act * gelu_slope(jnp.concatenate(old, axis=0))
    summed = scatter_sum(product(d_pre, w_first, ((1,), (1,))), "tensor")
    moved_grad = moved(g_rows + summed, -1)

    given = None
    shape = (1, rows, width)
    spans = cuts(rows, NEW_EIGHTHS)
    last = len(spans) - 1
    flying = []
    for i, (at, size) in enumerate(spans):
        piece = pre[at : at + size]
        if i == 1:
            piece, _ = barrier((piece, old))
        elif i >= 2:
            place, part = flying[i - 2]
            given = put(given, part, place, shape)
            if i == last:
                piece, given, moved_out, moved_grad = barrier((piece, given, moved_out, moved_grad))
            else:
                piece, given = barrier((piece, given))
        flying.append((at, across(piece, "section", mask)))
    for place, part in flying[-2:]:
        given = put(given, part, place, shape)
    return (moved_out[None], moved_grad[None], given)


def solution(mesh):
    return jax.shard_map(
        shards,
        mesh=mesh,
        in_specs=(
            P("section", "tensor", None),
            P("section", "tensor", None),
            P("section", None, "tensor"),
            P("section", "tensor", None),
            P("section", None, "tensor"),
        ),
        out_specs=(
            P("section", "tensor", None),
            P("section", "tensor", None),
            P("section", None, "tensor"),
        ),
        check_vma=False,
    )
```

time: 390 us -> 406 us (1.041)
  the two profiles are of different devices: /device:TPU:1 before, /device:TPU:0 now
where the time goes in v1:
time: 406 us
  waiting for transfers between devices  241 us (59%)
  matrix products  70.1 us (17%)
  starting transfers between devices  56.5 us (14%)
  local copies, waits for them, and re-layouts  26 us (6%)
  Pallas kernels  8.8 us (2%)
    ppermute x17, waiting for transfers between devices, across(): return lax.ppermute(value, axis, pairs)  213 us
    dot_general x4, matrix products, product(): lax.dot_general(left, right, (contract, ((), ())), precision=lax.Precisio...  70.1 us
    ppermute x17, starting transfers between devices, across(): return lax.ppermute(value, axis, pairs)  51.9 us
    ppermute x4, waiting for transfers between devices, from_behind(): lax.ppermute(value, axis, [(i, (i + by) % length) for i in range(length)])  27.4 us
    unnamed x38, local copies, waits for them, and re-layouts  10.9 us
    pallas_call x4, Pallas kernels, put(): pl.pallas_call(functools.partial(put_kernel, at), out_shape=jax.ShapeDtyp...  8.8 us
  transfers between devices with their start and end apart: 21, of which 14 were waited for; matrix products, arithmetic and copies ran while one was open for 23% of the time, Pallas kernels for 2%

profile of v1, /device:TPU:0, one launch (start us, length us, event | category | flops | bytes accessed | tf_op | source)
XLA Modules:
  0.0 405.8 jit_solution(7749441822501610963)
XLA Ops:
  0.6 1.1 constant_dynamic-update-slice_fusion.1
  1.8 1.2 constant_dynamic-update-slice_fusion
  2.9 3.0 collective-permute-start
  6.0 1.5 collective-permute-start.1
  7.5 1.9 slice_bitcast_fusion.4
  9.4 2.7 slice.52
  12.1 3.0 collective-permute-start.5
  15.2 1.5 fusion.26
  16.6 0.2 broadcast_in_dim.9
  16.9 0.1 constant_dynamic-update-slice_fusion.9
  16.9 1.8 collective-permute-done
  18.7 3.1 collective-permute-start.6
  21.9 8.7 %collective-permute-done.1 = f32[2,64,1024]{2,1,0:T(8,128)S(1)} collective-permute-done((f32[2,64,1024]{2,1,0:T(8,128)S(1)}, f32[2,64,1024]{2,1,0:T(8,128)S(1)}, u32[]{:S(2)}, u32[]{:S(2)}) %collective-permute-start.1) | collective-permute-done | bytes 524320 | tf_op jit(solution)/shard_map/ppermute | solution.py:17
  30.6 2.6 collective-permute-start.7
  33.2 0.1 constant_dynamic-update-slice_fusion.6
  33.3 1.3 copy-done.1
  34.7 17.4 %fusion.6 = f32[256,4096]{1,0:T(8,128)S(1)} fusion(f32[1,1024,4096]{2,1,0:T(8,128)} %param.7, f32[2,256,1024]{2,1,0:T(8,128)S(1)} %constant_dynamic-update-slice_fusion.6), kind=kOutput, calls=%fused_computation.6 | convolution fusion | flops 12884901888 | bytes 22020096 | tf_op jit(solution)/shard_map/dot_general | solution.py:36
  52.1 16.1 %fusion.2 = f32[256,1024]{1,0:T(8,128)} fusion(f32[1,4096,1024]{2,1,0:T(8,128)S(1)} %bitcast.31, f32[256,4096]{1,0:T(8,128)S(1)} %fusion.6), kind=kOutput, calls=%fused_computation.2 | convolution fusion | flops 12889096192 | bytes 22020096 | tf_op jit(solution)/shard_map/dot_general | solution.py:36
  68.2 1.3 slice.63
  69.5 0.3 collective-permute-start.3
  69.8 115.2 %collective-permute-done.4 = f32[32,4096]{1,0:T(8,128)} collective-permute-done((f32[32,4096]{1,0:T(8,128)}, f32[32,4096]{1,0:T(8,128)}, u32[]{:S(2)}, u32[]{:S(2)}) %collective-permute-start.4) | collective-permute-done | bytes 524320 | tf_op jit(solution)/shard_map/ppermute | solution.py:17
  185.0 1.9 constant_dynamic-update-slice_fusion.5
  186.9 2.7 constant_dynamic-update-slice_fusion.4
  189.5 17.8 %collective-permute-done.6 = f32[64,4096]{1,0:T(8,128)S(1)} collective-permute-done((f32[64,4096]{1,0:T(8,128)}, f32[64,4096]{1,0:T(8,128)S(1)}, u32[]{:S(2)}, u32[]{:S(2)}) %collective-permute-start.6) | collective-permute-done | bytes 1048608 | tf_op jit(solution)/shard_map/ppermute | solution.py:17
  207.4 1.0 constant_dynamic-update-slice_fusion.3
  208.4 21.5 %collective-permute-done.7 = f32[64,4096]{1,0:T(8,128)} collective-permute-done((f32[64,4096]{1,0:T(8,128)}, f32[64,4096]{1,0:T(8,128)}, u32[]{:S(2)}, u32[]{:S(2)}) %collective-permute-start.7) | collective-permute-done | bytes 1048608 | tf_op jit(solution)/shard_map/ppermute | solution.py:17
  229.9 2.3 constant_dynamic-update-slice_fusion.2
  232.2 20.1 %fusion.8 = f32[256,4096]{1,0:T(8,128)} fusion(f32[1,4096,1024]{2,1,0:T(8,128)} %param.8, f32[256,4096]{1,0:T(8,128)} %constant_dynamic-update-slice_fusion.2, f32[2,256,1024]{2,1,0:T(8,128)} %copy-done.1), kind=kOutput, calls=%fused_computation.9 | convolution fusion | flops 12894339072 | bytes 26214400 | tf_op jit(solution)/shard_map/dot_general | solution.py:36
  252.4 16.6 %fusion.4 = f32[256,1024]{1,0:T(8,128)S(1)} fusion(f32[256,4096]{1,0:T(8,128)} %fusion.8, f32[1,1024,4096]{2,1,0:T(8,128)S(1)} %bitcast.29), kind=kOutput, calls=%fused_computation.4 | convolution fusion | flops 12884901888 | bytes 22020096 | tf_op jit(solution)/shard_map/dot_general | solution.py:36
  269.0 0.2 constant_dynamic-slice_fusion.2
  269.2 1.6 collective-permute-start.14
  270.7 1.5 collective-permute-start.15
  272.2 0.5 collective-permute-start.16
  272.7 1.1 fusion.27
  273.9 1.5 collective-permute-start.10
  275.4 3.0 collective-permute-done.14
  278.4 2.4 collective-permute-start.11
  280.8 9.7 %collective-permute-done.15 = f32[64,1024]{1,0:T(8,128)S(1)} collective-permute-done((f32[64,1024]{1,0:T(8,128)S(1)}, f32[64,1024]{1,0:T(8,128)S(1)}, u32[]{:S(2)}, u32[]{:S(2)}) %collective-permute-start.15) | collective-permute-done | bytes 262176 | tf_op jit(solution)/shard_map/ppermute | solution.py:17
  290.6 0.3 collective-permute-start.9
  290.9 0.1 bitcast_add_fusion
  291.0 0.7 fusion.28
  291.7 1.7 collective-permute-done.10
  293.4 2.9 collective-permute-start.17
  296.3 1.7 collective-permute-start.18
  298.0 0.1 bitcast_add_fusion.1
  298.1 2.6 shard_map.76.refs_0_
  300.7 0.1 collective-permute-start.19
  300.8 0.1 collective-permute-start.12
  300.9 9.1 %collective-permute-done.17 = f32[32,1024]{1,0:T(8,128)S(1)} collective-permute-done((f32[32,1024]{1,0:T(8,128)}, f32[32,1024]{1,0:T(8,128)S(1)}, u32[]{:S(2)}, u32[]{:S(2)}) %collective-permute-start.17) | collective-permute-done | bytes 131104 | tf_op jit(solution)/shard_map/ppermute | solution.py:22
  309.9 1.9 slice.61
  311.8 0.9 collective-permute-done.18
  312.7 14.6 %collective-permute-done.12 = f32[32,1024]{1,0:T(8,128)S(1)} collective-permute-done((f32[32,1024]{1,0:T(8,128)S(1)}, f32[32,1024]{1,0:T(8,128)S(1)}, u32[]{:S(2)}, u32[]{:S(2)}) %collective-permute-start.12) | collective-permute-done | bytes 131104 | tf_op jit(solution)/shard_map/ppermute | solution.py:22
  327.3 2.8 collective-permute-done.13
  330.1 1.6 pad_maximum_fusion.1
  331.7 0.7 pad_maximum_fusion
  332.5 24.4 %collective-permute-done.8.refs_1_ = f32[64,4096]{1,0:T(8,128)S(1)} collective-permute-done((f32[64,4096]{1,0:T(8,128)}, f32[64,4096]{1,0:T(8,128)S(1)}, u32[]{:S(2)}, u32[]{:S(2)}) %collective-permute-start.8) | collective-permute-done | bytes 1048608 | tf_op jit(solution)/shard_map/ppermute | solution.py:17
  356.9 1.0 copy-done.4
  357.9 2.2 shard_map.77.refs_0_
  360.1 30.3 %collective-permute-start.20 = (f32[32,4096]{1,0:T(8,128)}, f32[32,4096]{1,0:T(8,128)S(1)}, u32[]{:S(2)}, u32[]{:S(2)}) collective-permute-start(f32[32,4096]{1,0:T(8,128)} %slice.61), channel_id=1, source_target_pairs={{0,16},{4,20},{8,24},{12,28},{16,0},{20,4},{24,8},{28,12},{1,17},{... | collective-permute-start | bytes 1572872 | tf_op jit(solution)/shard_map/ppermute | solution.py:17
  390.4 1.0 copy-done.5
  391.4 2.2 shard_map.78.refs_0_
  393.6 9.4 %collective-permute-done.20.refs_1_ = f32[32,4096]{1,0:T(8,128)S(1)} collective-permute-done((f32[32,4096]{1,0:T(8,128)}, f32[32,4096]{1,0:T(8,128)S(1)}, u32[]{:S(2)}, u32[]{:S(2)}) %collective-permute-start.20) | collective-permute-done | bytes 524320 | tf_op jit(solution)/shard_map/ppermute | solution.py:17
  402.9 0.8 copy-done.8
  403.7 1.8 shard_map.79
  (46 shorter events, 0.3 us)
Async XLA Ops:
  0.6 14.5 %copy-start.2 = (f32[1,256,4096]{2,1,0:T(8,128)S(1)}, f32[1,256,4096]{2,1,0:T(8,128)}, u32[]{:S(2)}) copy-start(f32[1,256,4096]{2,1,0:T(8,128)} %param.9) | copy-start | bytes 12582916
  2.9 15.8 %collective-permute-start = (f32[2,64,1024]{2,1,0:T(8,128)S(1)}, f32[2,64,1024]{2,1,0:T(8,128)S(1)}, u32[]{:S(2)}, u32[]{:S(2)}) collective-permute-start(f32[2,64,1024]{2,1,0:T(8,128)S(1)} %constant_dynamic-update-slice_fusion), channel_id=1, source_target_pairs={{0,1},{1,0},{2,3},{3,2},{4,5},{5,4},{6,7},{7,6},{8,9},{9,8},{10,11... | collective-permute-start | bytes 1572872 | tf_op jit(solution)/shard_map/ppermute | solution.py:17
  6.0 24.6 %collective-permute-start.1 = (f32[2,64,1024]{2,1,0:T(8,128)S(1)}, f32[2,64,1024]{2,1,0:T(8,128)S(1)}, u32[]{:S(2)}, u32[]{:S(2)}) collective-permute-start(f32[2,64,1024]{2,1,0:T(8,128)S(1)} %constant_dynamic-update-slice_fusion), channel_id=1, source_target_pairs={{0,2},{1,3},{2,0},{3,1},{4,6},{5,7},{6,4},{7,5},{8,10},{9,11},{10,... | collective-permute-start | bytes 1572872 | tf_op jit(solution)/shard_map/ppermute | solution.py:17
  7.5 25.7 %collective-permute-start.2 = (f32[2,64,1024]{2,1,0:T(8,128)S(1)}, f32[2,64,1024]{2,1,0:T(8,128)S(1)}, u32[]{:S(2)}, u32[]{:S(2)}) collective-permute-start(f32[2,64,1024]{2,1,0:T(8,128)S(1)} %constant_dynamic-update-slice_fusion), channel_id=1, source_target_pairs={{0,3},{1,2},{2,1},{3,0},{4,7},{5,6},{6,5},{7,4},{8,11},{9,10},{10,... | collective-permute-start | bytes 1572872 | tf_op jit(solution)/shard_map/ppermute | solution.py:17
  12.1 174.8 %collective-permute-start.5 = (f32[96,4096]{1,0:T(8,128)}, f32[96,4096]{1,0:T(8,128)}, u32[]{:S(2)}, u32[]{:S(2)}) collective-permute-start(f32[96,4096]{1,0:T(8,128)} %slice.52), channel_id=1, source_target_pairs={{0,16},{4,20},{8,24},{12,28},{16,0},{20,4},{24,8},{28,12},{1,17},{... | collective-permute-start | bytes 4718600 | tf_op jit(solution)/shard_map/ppermute | solution.py:17
  15.1 169.9 %collective-permute-start.4 = (f32[32,4096]{1,0:T(8,128)}, f32[32,4096]{1,0:T(8,128)}, u32[]{:S(2)}, u32[]{:S(2)}) collective-permute-start(f32[32,4096]{1,0:T(8,128)} %slice_bitcast_fusion.4), channel_id=1, source_target_pairs={{0,16},{4,20},{8,24},{12,28},{16,0},{20,4},{24,8},{28,12},{1,17},{... | collective-permute-start | bytes 1572872 | tf_op jit(solution)/shard_map/ppermute | solution.py:17
  16.9 35.2 %slice-start.4 = ((s8[16777216]{0:T(1024)(128)(4,1)}), s8[4194304]{0:T(1024)(128)(4,1)S(1)}, s32[]{:S(2)}) async-start(s8[16777216]{0:T(1024)(128)(4,1)} %bitcast.30), calls=%async_computation.4 | async-start | bytes 8388608
  18.7 188.6 %collective-permute-start.6 = (f32[64,4096]{1,0:T(8,128)}, f32[64,4096]{1,0:T(8,128)S(1)}, u32[]{:S(2)}, u32[]{:S(2)}) collective-permute-start(f32[64,4096]{1,0:T(8,128)} %get-tuple-element.30), channel_id=1, source_target_pairs={{0,16},{4,20},{8,24},{12,28},{16,0},{20,4},{24,8},{28,12},{1,17},{... | collective-permute-start | bytes 3145736 | tf_op jit(solution)/shard_map/ppermute | solution.py:17
  30.6 199.3 %collective-permute-start.7 = (f32[64,4096]{1,0:T(8,128)}, f32[64,4096]{1,0:T(8,128)}, u32[]{:S(2)}, u32[]{:S(2)}) collective-permute-start(f32[64,4096]{1,0:T(8,128)} %get-tuple-element.29), channel_id=1, source_target_pairs={{0,16},{4,20},{8,24},{12,28},{16,0},{20,4},{24,8},{28,12},{1,17},{... | collective-permute-start | bytes 3145736 | tf_op jit(solution)/shard_map/ppermute | solution.py:17
  33.3 1.4 copy-start.1
  34.7 17.4 %slice-start.5 = ((s8[16777216]{0:T(1024)(128)(4,1)}), s8[4194304]{0:T(1024)(128)(4,1)S(1)}, s32[]{:S(2)}) async-start(s8[16777216]{0:T(1024)(128)(4,1)} %bitcast.30), calls=%async_computation.5 | async-start | bytes 8388608
  34.7 17.4 %slice-start.6 = ((s8[16777216]{0:T(1024)(128)(4,1)}), s8[4194304]{0:T(1024)(128)(4,1)S(1)}, s32[]{:S(2)}) async-start(s8[16777216]{0:T(1024)(128)(4,1)} %bitcast.30), calls=%async_computation.6 | async-start | bytes 8388608
  34.7 17.4 %slice-start.7 = ((s8[16777216]{0:T(1024)(128)(4,1)}), s8[4194304]{0:T(1024)(128)(4,1)S(1)}, s32[]{:S(2)}) async-start(s8[16777216]{0:T(1024)(128)(4,1)} %bitcast.30), calls=%async_computation.7 | async-start | bytes 8388608
  52.1 220.6 %copy-start = (f32[256,4096]{1,0:T(8,128)}, f32[256,4096]{1,0:T(8,128)S(1)}, u32[]{:S(2)}) copy-start(f32[256,4096]{1,0:T(8,128)S(1)} %fusion.6) | copy-start | bytes 12582916
  69.5 228.7 %collective-permute-start.3 = (f32[96,4096]{1,0:T(8,128)}, f32[96,4096]{1,0:T(8,128)}, u32[]{:S(2)}, u32[]{:S(2)}) collective-permute-start(f32[96,4096]{1,0:T(8,128)} %slice.63), channel_id=1, source_target_pairs={{0,16},{4,20},{8,24},{12,28},{16,0},{20,4},{24,8},{28,12},{1,17},{... | collective-permute-start | bytes 4718600 | tf_op jit(solution)/shard_map/ppermute | solution.py:17
  207.4 45.0 %slice-start = ((s8[16777216]{0:T(1024)(128)(4,1)}), s8[4194304]{0:T(1024)(128)(4,1)S(1)}, s32[]{:S(2)}) async-start(s8[16777216]{0:T(1024)(128)(4,1)} %bitcast.28), calls=%async_computation | async-start | bytes 8388608
  232.2 20.1 %slice-start.1 = ((s8[16777216]{0:T(1024)(128)(4,1)}), s8[4194304]{0:T(1024)(128)(4,1)S(1)}, s32[]{:S(2)}) async-start(s8[16777216]{0:T(1024)(128)(4,1)} %bitcast.28), calls=%async_computation.1 | async-start | bytes 8388608
  232.2 20.1 %slice-start.2 = ((s8[16777216]{0:T(1024)(128)(4,1)}), s8[4194304]{0:T(1024)(128)(4,1)S(1)}, s32[]{:S(2)}) async-start(s8[16777216]{0:T(1024)(128)(4,1)} %bitcast.28), calls=%async_computation.2 | async-start | bytes 8388608
  232.2 20.1 %slice-start.3 = ((s8[16777216]{0:T(1024)(128)(4,1)}), s8[4194304]{0:T(1024)(128)(4,1)S(1)}, s32[]{:S(2)}) async-start(s8[16777216]{0:T(1024)(128)(4,1)} %bitcast.28), calls=%async_computation.3 | async-start | bytes 8388608
  252.4 16.6 %copy-start.3 = (f32[256,1024]{1,0:T(8,128)S(1)}, f32[256,1024]{1,0:T(8,128)}, u32[]{:S(2)}) copy-start(f32[256,1024]{1,0:T(8,128)} %fusion.2) | copy-start | bytes 3145732
  268.9 22.0 %copy-start.6 = (f32[1,64,1024]{2,1,0:T(8,128)S(1)}, f32[1,64,1024]{2,1,0:T(8,128)}, u32[]{:S(2)}) copy-start(f32[1,64,1024]{2,1,0:T(8,128)} %param.6) | copy-start | bytes 786436
  269.0 29.1 %copy-start.7 = (f32[1,64,1024]{2,1,0:T(8,128)S(1)}, f32[1,64,1024]{2,1,0:T(8,128)}, u32[]{:S(2)}) copy-start(f32[1,64,1024]{2,1,0:T(8,128)} %param.5) | copy-start | bytes 786436
  269.2 9.2 %collective-permute-start.14 = (f32[64,1024]{1,0:T(8,128)S(1)}, f32[64,1024]{1,0:T(8,128)S(1)}, u32[]{:S(2)}, u32[]{:S(2)}) collective-permute-start(f32[64,1024]{1,0:T(8,128)S(1)} %get-tuple-element.33), channel_id=1, source_target_pairs={{0,1},{1,0},{2,3},{3,2},{4,5},{5,4},{6,7},{7,6},{8,9},{9,8},{10,11... | collective-permute-start | bytes 786440 | tf_op jit(solution)/shard_map/ppermute | solution.py:17
  270.7 19.9 %collective-permute-start.15 = (f32[64,1024]{1,0:T(8,128)S(1)}, f32[64,1024]{1,0:T(8,128)S(1)}, u32[]{:S(2)}, u32[]{:S(2)}) collective-permute-start(f32[64,1024]{1,0:T(8,128)S(1)} %get-tuple-element.35), channel_id=1, source_target_pairs={{0,2},{1,3},{2,0},{3,1},{4,6},{5,7},{6,4},{7,5},{8,10},{9,11},{10,... | collective-permute-start | bytes 786440 | tf_op jit(solution)/shard_map/ppermute | solution.py:17
  272.2 18.7 %collective-permute-start.16 = (f32[64,1024]{1,0:T(8,128)S(1)}, f32[64,1024]{1,0:T(8,128)S(1)}, u32[]{:S(2)}, u32[]{:S(2)}) collective-permute-start(f32[64,1024]{1,0:T(8,128)S(1)} %get-tuple-element.34), channel_id=1, source_target_pairs={{0,3},{1,2},{2,1},{3,0},{4,7},{5,6},{6,5},{7,4},{8,11},{9,10},{10,... | collective-permute-start | bytes 786440 | tf_op jit(solution)/shard_map/ppermute | solution.py:17
  273.9 19.5 %collective-permute-start.10 = (f32[64,1024]{1,0:T(8,128)S(1)}, f32[64,1024]{1,0:T(8,128)S(1)}, u32[]{:S(2)}, u32[]{:S(2)}) collective-permute-start(f32[64,1024]{1,0:T(8,128)S(1)} %get-tuple-element.43), channel_id=1, source_target_pairs={{0,2},{1,3},{2,0},{3,1},{4,6},{5,7},{6,4},{7,5},{8,10},{9,11},{10,... | collective-permute-start | bytes 786440 | tf_op jit(solution)/shard_map/ppermute | solution.py:17
  278.4 17.9 %collective-permute-start.11 = (f32[64,1024]{1,0:T(8,128)S(1)}, f32[64,1024]{1,0:T(8,128)S(1)}, u32[]{:S(2)}, u32[]{:S(2)}) collective-permute-start(f32[64,1024]{1,0:T(8,128)S(1)} %get-tuple-element.44), channel_id=1, source_target_pairs={{0,3},{1,2},{2,1},{3,0},{4,7},{5,6},{6,5},{7,4},{8,11},{9,10},{10,... | collective-permute-start | bytes 786440 | tf_op jit(solution)/shard_map/ppermute | solution.py:17
  290.6 7.4 %collective-permute-start.9 = (f32[64,1024]{1,0:T(8,128)S(1)}, f32[64,1024]{1,0:T(8,128)S(1)}, u32[]{:S(2)}, u32[]{:S(2)}) collective-permute-start(f32[64,1024]{1,0:T(8,128)S(1)} %get-tuple-element.45), channel_id=1, source_target_pairs={{0,1},{1,0},{2,3},{3,2},{4,5},{5,4},{6,7},{7,6},{8,9},{9,8},{10,11... | collective-permute-start | bytes 786440 | tf_op jit(solution)/shard_map/ppermute | solution.py:17
  290.9 66.0 %collective-permute-start.8 = (f32[64,4096]{1,0:T(8,128)}, f32[64,4096]{1,0:T(8,128)S(1)}, u32[]{:S(2)}, u32[]{:S(2)}) collective-permute-start(f32[64,4096]{1,0:T(8,128)} %get-tuple-element.19), channel_id=1, source_target_pairs={{0,16},{4,20},{8,24},{12,28},{16,0},{20,4},{24,8},{28,12},{1,17},{... | collective-permute-start | bytes 3145736 | tf_op jit(solution)/shard_map/ppermute | solution.py:17
  293.4 16.5 %collective-permute-start.17 = (f32[32,1024]{1,0:T(8,128)}, f32[32,1024]{1,0:T(8,128)S(1)}, u32[]{:S(2)}, u32[]{:S(2)}) collective-permute-start(f32[32,1024]{1,0:T(8,128)} %get-tuple-element.40), channel_id=1, source_target_pairs={{0,28},{4,0},{8,4},{12,8},{16,12},{20,16},{24,20},{28,24},{1,29},{... | collective-permute-start | bytes 393224 | tf_op jit(solution)/shard_map/ppermute | solution.py:22
  296.3 16.4 %collective-permute-start.18 = (f32[32,1024]{1,0:T(8,128)}, f32[32,1024]{1,0:T(8,128)}, u32[]{:S(2)}, u32[]{:S(2)}) collective-permute-start(f32[32,1024]{1,0:T(8,128)} %get-tuple-element.39), channel_id=1, source_target_pairs={{0,28},{4,0},{8,4},{12,8},{16,12},{20,16},{24,20},{28,24},{1,29},{... | collective-permute-start | bytes 393224 | tf_op jit(solution)/shard_map/ppermute | solution.py:22
  300.7 89.7 %collective-permute-start.19 = (f32[64,4096]{1,0:T(8,128)S(1)}, f32[64,4096]{1,0:T(8,128)S(1)}, u32[]{:S(2)}, u32[]{:S(2)}) collective-permute-start(f32[64,4096]{1,0:T(8,128)S(1)} %get-tuple-element.27), channel_id=1, source_target_pairs={{0,16},{4,20},{8,24},{12,28},{16,0},{20,4},{24,8},{28,12},{1,17},{... | collective-permute-start | bytes 3145736 | tf_op jit(solution)/shard_map/ppermute | solution.py:17
  300.8 26.5 %collective-permute-start.12 = (f32[32,1024]{1,0:T(8,128)S(1)}, f32[32,1024]{1,0:T(8,128)S(1)}, u32[]{:S(2)}, u32[]{:S(2)}) collective-permute-start(f32[32,1024]{1,0:T(8,128)S(1)} %get-tuple-element.42), channel_id=1, source_target_pairs={{0,4},{4,8},{8,12},{12,16},{16,20},{20,24},{24,28},{28,0},{1,5},{5... | collective-permute-start | bytes 393224 | tf_op jit(solution)/shard_map/ppermute | solution.py:22
  309.9 20.2 %collective-permute-start.13 = (f32[32,1024]{1,0:T(8,128)S(1)}, f32[32,1024]{1,0:T(8,128)S(1)}, u32[]{:S(2)}, u32[]{:S(2)}) collective-permute-start(f32[32,1024]{1,0:T(8,128)S(1)} %get-tuple-element.41), channel_id=1, source_target_pairs={{0,4},{4,8},{8,12},{12,16},{16,20},{20,24},{24,28},{28,0},{1,5},{5... | collective-permute-start | bytes 393224 | tf_op jit(solution)/shard_map/ppermute | solution.py:22
  356.9 1.0 copy-start.4
  360.1 42.8 %collective-permute-start.20 = (f32[32,4096]{1,0:T(8,128)}, f32[32,4096]{1,0:T(8,128)S(1)}, u32[]{:S(2)}, u32[]{:S(2)}) collective-permute-start(f32[32,4096]{1,0:T(8,128)} %slice.61), channel_id=1, source_target_pairs={{0,16},{4,20},{8,24},{12,28},{16,0},{20,4},{24,8},{28,12},{1,17},{... | collective-permute-start | bytes 1572872 | tf_op jit(solution)/shard_map/ppermute | solution.py:17
  390.4 1.0 copy-start.5
  402.9 0.8 copy-start.8

commit v2 on v1

--- a/solution.py
+++ b/solution.py
@@ -8,8 +8,7 @@
 from jax.sharding import PartitionSpec as P
 
 
-OLD_EIGHTHS = (1, 3, 2, 2)
-NEW_EIGHTHS = (3, 2, 2, 1)
+NEW_EIGHTHS = (4, 3, 1)
 
 
 def across(value, axis, mask):
@@ -110,43 +109,36 @@
     rows, width = held.shape
     barrier = lax.optimization_barrier
 
-    old = []
-    for i, (at, size) in enumerate(cuts(rows, OLD_EIGHTHS)):
-        piece = held[at : at + size]
-        if i == 0:
-            piece, held = barrier((piece, held))
-        old.append(across(piece, "section", mask))
+    old_pre = across(held, "section", mask)
 
     both = gather_rows(jnp.stack([x_rows, g_rows]), "tensor")
+    x_all, g_all = both[0], both[1]
 
-    pre = product(both[0], w_first, ((1,), (0,)))
-    summed = scatter_sum(product(gelu_exact(pre), w_second, ((1,), (0,))), "tensor")
-    moved_out = moved(x_rows + summed, 1)
+    d_act = product(g_all, w_second, ((1,), (1,)))
+    x_all, d_act = barrier((x_all, d_act))
 
-    d_act = product(both[1], w_second, ((1,), (1,)))
-    d_pre = d_act * gelu_slope(jnp.concatenate(old, axis=0))
-    summed = scatter_sum(product(d_pre, w_first, ((1,), (1,))), "tensor")
-    moved_grad = moved(g_rows + summed, -1)
+    pre = product(x_all, w_first, ((1,), (0,)))
+    summed = product(gelu_exact(pre), w_second, ((1,), (0,)))
+    moved_out = moved(x_rows + scatter_sum(summed, "tensor"), 1)
 
-    given = None
-    shape = (1, rows, width)
     spans = cuts(rows, NEW_EIGHTHS)
-    last = len(spans) - 1
     flying = []
     for i, (at, size) in enumerate(spans):
         piece = pre[at : at + size]
-        if i == 1:
-            piece, _ = barrier((piece, old))
-        elif i >= 2:
-            place, part = flying[i - 2]
-            given = put(given, part, place, shape)
-            if i == last:
-                piece, given, moved_out, moved_grad = barrier((piece, given, moved_out, moved_grad))
-            else:
-                piece, given = barrier((piece, given))
+        if i >= 1:
+            piece, old_pre = barrier((piece, old_pre))
         flying.append((at, across(piece, "section", mask)))
-    for place, part in flying[-2:]:
-        given = put(given, part, place, shape)
+
+    d_pre = d_act * gelu_slope(old_pre)
+    summed = product(d_pre, w_first, ((1,), (1,)))
+    moved_grad = moved(g_rows + scatter_sum(summed, "tensor"), -1)
+
+    given = None
+    for place, part in flying[:-1]:
+        given = put(given, part, place, (1, rows, width))
+    given, moved_out, moved_grad = barrier((given, moved_out, moved_grad))
+    place, part = flying[-1]
+    given = lax.dynamic_update_slice(given, part[None], (0, place, 0))
     return (moved_out[None], moved_grad[None], given)
 
 

time: 406 us -> 378 us (0.931)
  the two profiles are of different devices: /device:TPU:0 before, /device:TPU:9 now
where the time goes in v2:
time: 378 us
  waiting for transfers between devices  255 us (67%)
  matrix products  89.5 us (24%)
  starting transfers between devices  16.1 us (4%)
  local copies, waits for them, and re-layouts  8.15 us (2%)
  Pallas kernels  5.47 us (1%)
    ppermute x13, waiting for transfers between devices, across(): return lax.ppermute(value, axis, pairs)  209 us
    dot_general x4, matrix products, product(): lax.dot_general(left, right, (contract, ((), ())), precision=lax.Precisio...  89.5 us
    ppermute x4, waiting for transfers between devices, from_behind(): lax.ppermute(value, axis, [(i, (i + by) % length) for i in range(length)])  45.9 us
    ppermute x13, starting transfers between devices, across(): return lax.ppermute(value, axis, pairs)  14.3 us
  transfers between devices with their start and end apart: 17, of which 7 were waited for; matrix products, arithmetic and copies ran while one was open for 26% of the time, Pallas kernels for 1%

profile of v2, /device:TPU:9, one launch (start us, length us, event | category | flops | bytes accessed | tf_op | source)
XLA Modules:
  0.0 377.9 jit_solution(17570047883761208196)
XLA Ops:
  0.6 1.0 constant_dynamic-update-slice_fusion.1
  1.6 1.0 constant_dynamic-update-slice_fusion
  2.6 1.3 collective-permute-start
  3.9 2.3 collective-permute-start.4
  6.2 1.2 collective-permute-start.1
  7.4 0.2 collective-permute-start.2
  7.6 0.2 broadcast_in_dim.12
  7.9 0.1 constant_dynamic-update-slice_fusion.5
  7.9 7.6 %collective-permute-done = f32[2,64,1024]{2,1,0:T(8,128)S(1)} collective-permute-done((f32[2,64,1024]{2,1,0:T(8,128)S(1)}, f32[2,64,1024]{2,1,0:T(8,128)S(1)}, u32[]{:S(2)}, u32[]{:S(2)}) %collective-permute-start) | collective-permute-done | bytes 524320 | tf_op jit(solution)/shard_map/ppermute | solution.py:16
  15.6 14.1 %collective-permute-done.1 = f32[2,64,1024]{2,1,0:T(8,128)S(1)} collective-permute-done((f32[2,64,1024]{2,1,0:T(8,128)S(1)}, f32[2,64,1024]{2,1,0:T(8,128)S(1)}, u32[]{:S(2)}, u32[]{:S(2)}) %collective-permute-start.1) | collective-permute-done | bytes 524320 | tf_op jit(solution)/shard_map/ppermute | solution.py:16
  29.8 0.0 collective-permute-done.2
  29.8 0.1 constant_dynamic-update-slice_fusion.2
  29.9 0.0 slice-start.1
  29.9 0.1 slice_bitcast_fusion.2
  30.0 0.0 slice-start.2
  30.0 0.0 slice-start.3
  30.0 18.2 %fusion.6 = f32[256,4096]{1,0:T(8,128)} fusion(f32[1,4096,1024]{2,1,0:T(8,128)} %param.8, f32[2,256,1024]{2,1,0:T(8,128)S(1)} %constant_dynamic-update-slice_fusion.2), kind=kOutput, calls=%fused_computation.6 | convolution fusion | flops 12884901888 | bytes 22020096 | tf_op jit(solution)/shard_map/dot_general | solution.py:35
  48.2 0.0 slice-done
  48.2 0.0 slice-done.1
  48.2 0.0 slice-done.2
  48.2 0.0 slice-done.3
  48.2 15.0 %fusion.2 = f32[256,4096]{1,0:T(8,128)S(1)} fusion(f32[256,1024]{1,0:T(8,128)S(1)} %slice_bitcast_fusion.2, f32[1,1024,4096]{2,1,0:T(8,128)S(1)} %bitcast.26), kind=kOutput, calls=%fused_computation.2 | convolution fusion | flops 12884901888 | bytes 22020096 | tf_op jit(solution)/shard_map/dot_general | solution.py:35
  63.2 1.3 slice.39
  64.5 0.9 slice.42
  65.4 1.5 slice.38
  66.9 19.2 %fusion.4 = f32[256,1024]{1,0:T(8,128)S(1)} fusion(f32[1,4096,1024]{2,1,0:T(8,128)} %param.8, f32[256,4096]{1,0:T(8,128)S(1)} %fusion.2), kind=kOutput, calls=%fused_computation.4 | convolution fusion | flops 12889096192 | bytes 22020096 | tf_op jit(solution)/shard_map/dot_general | solution.py:35
  86.1 0.0 copy-start
  86.1 1.0 constant_dynamic-slice_fusion.5
  87.1 0.0 collective-permute-start.6
  87.1 1.5 collective-permute-start.7
  88.6 1.2 collective-permute-start.8
  89.7 0.2 collective-permute-start.3
  89.9 141.6 %collective-permute-done.4 = f32[256,4096]{1,0:T(8,128)} collective-permute-done((f32[256,4096]{1,0:T(8,128)}, f32[256,4096]{1,0:T(8,128)}, u32[]{:S(2)}, u32[]{:S(2)}) %collective-permute-start.4) | collective-permute-done | bytes 4194336 | tf_op jit(solution)/shard_map/ppermute | solution.py:16
  231.5 0.0 copy-done
  231.5 3.1 collective-permute-start.5
  234.6 37.1 %fusion = f32[256,1024]{1,0:T(8,128)S(1)} fusion(f32[1,1024,4096]{2,1,0:T(8,128)S(1)} %bitcast.26, f32[256,4096]{1,0:T(8,128)} %fusion.6, f32[256,4096]{1,0:T(8,128)} %collective-permute-done.4), kind=kOutput, calls=%fused_computation | convolution fusion | flops 12894339072 | bytes 26214400 | tf_op jit(solution)/shard_map/dot_general | solution.py:35
  271.7 0.1 constant_dynamic-slice_fusion.2
  271.8 0.0 collective-permute-done.6
  271.8 0.3 collective-permute-start.11
  272.2 0.0 collective-permute-done.7
  272.2 1.2 collective-permute-start.12
  273.4 0.0 collective-permute-done.8
  273.4 1.2 collective-permute-start.13
  274.6 4.3 %collective-permute-done.11 = f32[64,1024]{1,0:T(8,128)S(1)} collective-permute-done((f32[64,1024]{1,0:T(8,128)S(1)}, f32[64,1024]{1,0:T(8,128)S(1)}, u32[]{:S(2)}, u32[]{:S(2)}) %collective-permute-start.11) | collective-permute-done | bytes 262176 | tf_op jit(solution)/shard_map/ppermute | solution.py:16
  278.9 0.6 collective-permute-start.16
  279.5 0.0 collective-permute-done.12
  279.5 6.0 %collective-permute-done.13 = f32[64,1024]{1,0:T(8,128)S(1)} collective-permute-done((f32[64,1024]{1,0:T(8,128)S(1)}, f32[64,1024]{1,0:T(8,128)S(1)}, u32[]{:S(2)}, u32[]{:S(2)}) %collective-permute-start.13) | collective-permute-done | bytes 262176 | tf_op jit(solution)/shard_map/ppermute | solution.py:16
  285.5 1.6 bitcast_add_fusion
  287.1 1.8 collective-permute-start.14
  288.8 0.1 collective-permute-start.15
  288.9 35.3 %collective-permute-done.3.refs_0_ = f32[128,4096]{1,0:T(8,128)} collective-permute-done((f32[128,4096]{1,0:T(8,128)}, f32[128,4096]{1,0:T(8,128)}, u32[]{:S(2)}, u32[]{:S(2)}) %collective-permute-start.3) | collective-permute-done | bytes 2097184 | tf_op jit(solution)/shard_map/ppermute | solution.py:16
  324.2 0.0 collective-permute-start.10
  324.2 45.9 %collective-permute-done.14 = f32[32,1024]{1,0:T(8,128)S(1)} collective-permute-done((f32[32,1024]{1,0:T(8,128)S(1)}, f32[32,1024]{1,0:T(8,128)S(1)}, u32[]{:S(2)}, u32[]{:S(2)}) %collective-permute-start.14) | collective-permute-done | bytes 131104 | tf_op jit(solution)/shard_map/ppermute | solution.py:21
  370.1 0.0 collective-permute-start.9
  370.1 2.9 shard_map.76.refs_0_
  373.0 0.0 collective-permute-done.15
  373.0 0.0 collective-permute-done.10
  373.1 0.0 collective-permute-done.9
  373.1 0.7 pad_maximum_fusion.1
  373.8 0.7 pad_maximum_fusion
  374.5 0.0 collective-permute-done.5.refs_1_
  374.5 2.6 shard_map.77
  377.1 0.0 collective-permute-done.16
  377.1 0.8 bitcast_dynamic-update-slice_fusion
  (6 shorter events, 0.1 us)
Async XLA Ops:
  2.6 13.0 %collective-permute-start = (f32[2,64,1024]{2,1,0:T(8,128)S(1)}, f32[2,64,1024]{2,1,0:T(8,128)S(1)}, u32[]{:S(2)}, u32[]{:S(2)}) collective-permute-start(f32[2,64,1024]{2,1,0:T(8,128)S(1)} %constant_dynamic-update-slice_fusion), channel_id=1, source_target_pairs={{0,1},{1,0},{2,3},{3,2},{4,5},{5,4},{6,7},{7,6},{8,9},{9,8},{10,11... | collective-permute-start | bytes 1572872 | tf_op jit(solution)/shard_map/ppermute | solution.py:16
  3.9 227.6 %collective-permute-start.4 = (f32[256,4096]{1,0:T(8,128)}, f32[256,4096]{1,0:T(8,128)}, u32[]{:S(2)}, u32[]{:S(2)}) collective-permute-start(f32[256,4096]{1,0:T(8,128)} %bitcast.29), channel_id=1, source_target_pairs={{0,16},{4,20},{8,24},{12,28},{16,0},{20,4},{24,8},{28,12},{1,17},{... | collective-permute-start | bytes 12582920 | tf_op jit(solution)/shard_map/ppermute | solution.py:16
  6.2 23.6 %collective-permute-start.1 = (f32[2,64,1024]{2,1,0:T(8,128)S(1)}, f32[2,64,1024]{2,1,0:T(8,128)S(1)}, u32[]{:S(2)}, u32[]{:S(2)}) collective-permute-start(f32[2,64,1024]{2,1,0:T(8,128)S(1)} %constant_dynamic-update-slice_fusion), channel_id=1, source_target_pairs={{0,2},{1,3},{2,0},{3,1},{4,6},{5,7},{6,4},{7,5},{8,10},{9,11},{10,... | collective-permute-start | bytes 1572872 | tf_op jit(solution)/shard_map/ppermute | solution.py:16
  7.4 22.4 %collective-permute-start.2 = (f32[2,64,1024]{2,1,0:T(8,128)S(1)}, f32[2,64,1024]{2,1,0:T(8,128)S(1)}, u32[]{:S(2)}, u32[]{:S(2)}) collective-permute-start(f32[2,64,1024]{2,1,0:T(8,128)S(1)} %constant_dynamic-update-slice_fusion), channel_id=1, source_target_pairs={{0,3},{1,2},{2,1},{3,0},{4,7},{5,6},{6,5},{7,4},{8,11},{9,10},{10,... | collective-permute-start | bytes 1572872 | tf_op jit(solution)/shard_map/ppermute | solution.py:16
  7.6 40.6 %slice-start = ((s8[16777216]{0:T(1024)(128)(4,1)}), s8[4194304]{0:T(1024)(128)(4,1)S(1)}, s32[]{:S(2)}) async-start(s8[16777216]{0:T(1024)(128)(4,1)} %bitcast.25), calls=%async_computation | async-start | bytes 8388608
  29.9 18.3 %slice-start.1 = ((s8[16777216]{0:T(1024)(128)(4,1)}), s8[4194304]{0:T(1024)(128)(4,1)S(1)}, s32[]{:S(2)}) async-start(s8[16777216]{0:T(1024)(128)(4,1)} %bitcast.25), calls=%async_computation.1 | async-start | bytes 8388608
  30.0 18.2 %slice-start.2 = ((s8[16777216]{0:T(1024)(128)(4,1)}), s8[4194304]{0:T(1024)(128)(4,1)S(1)}, s32[]{:S(2)}) async-start(s8[16777216]{0:T(1024)(128)(4,1)} %bitcast.25), calls=%async_computation.2 | async-start | bytes 8388608
  30.0 18.2 %slice-start.3 = ((s8[16777216]{0:T(1024)(128)(4,1)}), s8[4194304]{0:T(1024)(128)(4,1)S(1)}, s32[]{:S(2)}) async-start(s8[16777216]{0:T(1024)(128)(4,1)} %bitcast.25), calls=%async_computation.3 | async-start | bytes 8388608
  86.1 145.4 %copy-start = (f32[256,1024]{1,0:T(8,128)}, f32[256,1024]{1,0:T(8,128)S(1)}, u32[]{:S(2)}) copy-start(f32[256,1024]{1,0:T(8,128)S(1)} %fusion.4) | copy-start | bytes 3145732
  87.1 184.7 %collective-permute-start.6 = (f32[64,1024]{1,0:T(8,128)}, f32[64,1024]{1,0:T(8,128)}, u32[]{:S(2)}, u32[]{:S(2)}) collective-permute-start(f32[64,1024]{1,0:T(8,128)} %get-tuple-element.32), channel_id=1, source_target_pairs={{0,1},{1,0},{2,3},{3,2},{4,5},{5,4},{6,7},{7,6},{8,9},{9,8},{10,11... | collective-permute-start | bytes 786440 | tf_op jit(solution)/shard_map/ppermute | solution.py:16
  87.1 185.1 %collective-permute-start.7 = (f32[64,1024]{1,0:T(8,128)}, f32[64,1024]{1,0:T(8,128)}, u32[]{:S(2)}, u32[]{:S(2)}) collective-permute-start(f32[64,1024]{1,0:T(8,128)} %get-tuple-element.34), channel_id=1, source_target_pairs={{0,2},{1,3},{2,0},{3,1},{4,6},{5,7},{6,4},{7,5},{8,10},{9,11},{10,... | collective-permute-start | bytes 786440 | tf_op jit(solution)/shard_map/ppermute | solution.py:16
  88.6 184.8 %collective-permute-start.8 = (f32[64,1024]{1,0:T(8,128)}, f32[64,1024]{1,0:T(8,128)}, u32[]{:S(2)}, u32[]{:S(2)}) collective-permute-start(f32[64,1024]{1,0:T(8,128)} %get-tuple-element.33), channel_id=1, source_target_pairs={{0,3},{1,2},{2,1},{3,0},{4,7},{5,6},{6,5},{7,4},{8,11},{9,10},{10,... | collective-permute-start | bytes 786440 | tf_op jit(solution)/shard_map/ppermute | solution.py:16
  89.7 234.4 %collective-permute-start.3 = (f32[128,4096]{1,0:T(8,128)}, f32[128,4096]{1,0:T(8,128)}, u32[]{:S(2)}, u32[]{:S(2)}) collective-permute-start(f32[128,4096]{1,0:T(8,128)} %slice.38), channel_id=1, source_target_pairs={{0,16},{4,20},{8,24},{12,28},{16,0},{20,4},{24,8},{28,12},{1,17},{... | collective-permute-start | bytes 6291464 | tf_op jit(solution)/shard_map/ppermute | solution.py:16
  231.5 143.0 %collective-permute-start.5 = (f32[96,4096]{1,0:T(8,128)}, f32[96,4096]{1,0:T(8,128)}, u32[]{:S(2)}, u32[]{:S(2)}) collective-permute-start(f32[96,4096]{1,0:T(8,128)} %slice.39), channel_id=1, source_target_pairs={{0,16},{4,20},{8,24},{12,28},{16,0},{20,4},{24,8},{28,12},{1,17},{... | collective-permute-start | bytes 4718600 | tf_op jit(solution)/shard_map/ppermute | solution.py:16
  271.8 7.1 %collective-permute-start.11 = (f32[64,1024]{1,0:T(8,128)S(1)}, f32[64,1024]{1,0:T(8,128)S(1)}, u32[]{:S(2)}, u32[]{:S(2)}) collective-permute-start(f32[64,1024]{1,0:T(8,128)S(1)} %get-tuple-element.29), channel_id=1, source_target_pairs={{0,1},{1,0},{2,3},{3,2},{4,5},{5,4},{6,7},{7,6},{8,9},{9,8},{10,11... | collective-permute-start | bytes 786440 | tf_op jit(solution)/shard_map/ppermute | solution.py:16
  272.2 7.3 %collective-permute-start.12 = (f32[64,1024]{1,0:T(8,128)S(1)}, f32[64,1024]{1,0:T(8,128)S(1)}, u32[]{:S(2)}, u32[]{:S(2)}) collective-permute-start(f32[64,1024]{1,0:T(8,128)S(1)} %get-tuple-element.31), channel_id=1, source_target_pairs={{0,2},{1,3},{2,0},{3,1},{4,6},{5,7},{6,4},{7,5},{8,10},{9,11},{10,... | collective-permute-start | bytes 786440 | tf_op jit(solution)/shard_map/ppermute | solution.py:16
  273.4 12.1 %collective-permute-start.13 = (f32[64,1024]{1,0:T(8,128)S(1)}, f32[64,1024]{1,0:T(8,128)S(1)}, u32[]{:S(2)}, u32[]{:S(2)}) collective-permute-start(f32[64,1024]{1,0:T(8,128)S(1)} %get-tuple-element.30), channel_id=1, source_target_pairs={{0,3},{1,2},{2,1},{3,0},{4,7},{5,6},{6,5},{7,4},{8,11},{9,10},{10,... | collective-permute-start | bytes 786440 | tf_op jit(solution)/shard_map/ppermute | solution.py:16
  278.9 98.2 %collective-permute-start.16 = (f32[32,4096]{1,0:T(8,128)}, f32[32,4096]{1,0:T(8,128)S(1)}, u32[]{:S(2)}, u32[]{:S(2)}) collective-permute-start(f32[32,4096]{1,0:T(8,128)} %slice.42), channel_id=1, source_target_pairs={{0,16},{4,20},{8,24},{12,28},{16,0},{20,4},{24,8},{28,12},{1,17},{... | collective-permute-start | bytes 1572872 | tf_op jit(solution)/shard_map/ppermute | solution.py:16
  287.1 83.1 %collective-permute-start.14 = (f32[32,1024]{1,0:T(8,128)S(1)}, f32[32,1024]{1,0:T(8,128)S(1)}, u32[]{:S(2)}, u32[]{:S(2)}) collective-permute-start(f32[32,1024]{1,0:T(8,128)S(1)} %get-tuple-element.36), channel_id=1, source_target_pairs={{0,28},{4,0},{8,4},{12,8},{16,12},{20,16},{24,20},{28,24},{1,29},{... | collective-permute-start | bytes 393224 | tf_op jit(solution)/shard_map/ppermute | solution.py:21
  288.8 84.2 %collective-permute-start.15 = (f32[32,1024]{1,0:T(8,128)S(1)}, f32[32,1024]{1,0:T(8,128)S(1)}, u32[]{:S(2)}, u32[]{:S(2)}) collective-permute-start(f32[32,1024]{1,0:T(8,128)S(1)} %get-tuple-element.35), channel_id=1, source_target_pairs={{0,28},{4,0},{8,4},{12,8},{16,12},{20,16},{24,20},{28,24},{1,29},{... | collective-permute-start | bytes 393224 | tf_op jit(solution)/shard_map/ppermute | solution.py:21
  324.2 48.9 %collective-permute-start.10 = (f32[32,1024]{1,0:T(8,128)S(1)}, f32[32,1024]{1,0:T(8,128)S(1)}, u32[]{:S(2)}, u32[]{:S(2)}) collective-permute-start(f32[32,1024]{1,0:T(8,128)S(1)} %get-tuple-element.37), channel_id=1, source_target_pairs={{0,4},{4,8},{8,12},{12,16},{16,20},{20,24},{24,28},{28,0},{1,5},{5... | collective-permute-start | bytes 393224 | tf_op jit(solution)/shard_map/ppermute | solution.py:21
  370.1 3.0 collective-permute-start.9
